TPU v7x, 256 devices: a whole 4x4x8 slice. The times are simulated.
256 devices in a mesh: tm: 32 (over z, y_lo, core), gz: 8 (over y_hi, x).
Axes of the slice: x: 4, y: 4 (y_hi: 2, y_lo: 2; y = y_hi * 2 + y_lo), z: 8, core: 2. Of those that a mesh axis runs over, the one named last changes fastest.
Arguments:
- states: float32 [32, 4, 32, 128, 128], P('tm', None, 'gz'), may hold values from -6 to 6
- first_unconverged: int32 [1], replicated, may hold values from 0 to 31
- window_offset: int32 [1], replicated, may hold values from 0 to 63
- summaries: float32 [64], replicated, may hold values from -5 to 5
- cond_weight: float32 [64, 32], replicated, may hold values from -0.75 to 0.75
- time_gain: float32 [32], replicated, may hold values from -4 to 4
- conv_weight: float32 [27, 32, 4], replicated, may hold values from -0.625 to 0.625
- out_weight: float32 [4, 32], replicated, may hold values from -1 to 1
Outputs:
- new_states: float32 [32, 4, 32, 128, 128], P('tm', None, 'gz')
All inputs are finite; a program needn't handle non-finite values.
Results may differ from a plain program's by a relative error of at most 0.0001.
Values sent between devices are 32-bit elements; how exact they have to be, the bound alone decides.
A program may use at most 128 MiB of HBM per device.

v0:
```python
import jax
import jax.numpy as jnp
from jax import lax
from jax.sharding import PartitionSpec as P

STEP_SIZE = 0.125


def extended(block, sides, width):
    for axis, dim in sides:
        count = lax.axis_size(axis)
        forward = [(i, i + 1) for i in range(count - 1)]
        forward.append((count - 1, 0))
        backward = [(target, source) for source, target in forward]
        low = lax.ppermute(
            lax.slice_in_dim(block, block.shape[dim] - width, None, axis=dim), axis, forward
        )
        high = lax.ppermute(lax.slice_in_dim(block, 0, width, axis=dim), axis, backward)
        block = jnp.concatenate([low, block, high], axis=dim)
    return block


def carried_in(shard, axis, combine, identity):
    size, place = (lax.axis_size(axis), lax.axis_index(axis))
    everything = lax.all_gather(shard, axis)
    start = jnp.broadcast_to(jnp.asarray(identity, shard.dtype), shard.shape)

    def hop(k, before):
        reached = k < place
        new = combine(before, everything[k])
        return jnp.where(reached, new, before)

    return lax.fori_loop(0, size, hop, start)


def spread(shard, axis, root):
    mine = lax.axis_index(axis) == root
    return lax.psum(jnp.where(mine, shard, jnp.zeros_like(shard)), axis)


def shards(
    states,
    first_unconverged,
    window_offset,
    summaries,
    cond_weight,
    time_gain,
    conv_weight,
    out_weight,
):
    local_steps = states.shape[0]
    channels = states.shape[1]
    planes = states.shape[2]
    rows_y = states.shape[3]
    cols_x = states.shape[4]
    hidden_width = conv_weight.shape[1]
    all_steps = local_steps * lax.axis_size("tm")
    my_index = lax.axis_index("tm")
    global_steps = my_index * local_steps + jnp.arange(local_steps, dtype=jnp.int32)
    step_times = 1.0 - (window_offset[0] + global_steps).astype(jnp.float32) / float(all_steps + 64)
    condition = jnp.dot(
        summaries, cond_weight, precision=lax.Precision.HIGHEST, preferred_element_type=jnp.float32
    )
    stacked_weight = jnp.transpose(conv_weight, (1, 0, 2)).reshape(hidden_width, 27 * channels)
    padded = extended(states, (("gz", 2),), 1)

    def one_step(pair_item):
        state_block, step_time = pair_item
        offset_term = condition + step_time * time_gain

        def one_plane(plane_index):
            window_slab = lax.dynamic_slice_in_dim(state_block, plane_index, 3, 1)
            pieces = []
            for shift_z in (-1, 0, 1):
                for shift_y in (-1, 0, 1):
                    for shift_x in (-1, 0, 1):
                        pieces.append(
                            jnp.roll(window_slab[:, shift_z + 1], (-shift_y, -shift_x), axis=(1, 2))
                        )
            stacked = jnp.concatenate(pieces, axis=0).reshape(27 * channels, rows_y * cols_x)
            hidden = jnp.dot(
                stacked_weight,
                stacked,
                precision=lax.Precision.HIGHEST,
                preferred_element_type=jnp.float32,
            )
            activation = jax.nn.silu(hidden + offset_term[:, None])
            drift_plane = STEP_SIZE * jnp.dot(
                out_weight,
                activation,
                precision=lax.Precision.HIGHEST,
                preferred_element_type=jnp.float32,
            )
            return drift_plane.reshape(channels, rows_y, cols_x)

        drift_term = lax.map(one_plane, jnp.arange(planes, dtype=jnp.int32))
        return jnp.transpose(drift_term, (1, 0, 2, 3))

    increments = lax.map(one_step, (padded, step_times))
    running = jnp.cumsum(increments, axis=0)
    local_before = running - increments
    earlier_sum = carried_in(
        running[-1], "tm", lambda earlier, later: earlier + later, jnp.zeros_like(running[-1])
    )
    prefix = earlier_sum[None] + local_before
    root_device = first_unconverged[0] // local_steps
    local_row = first_unconverged[0] % local_steps
    picked = lax.dynamic_index_in_dim(states, local_row, 0, keepdims=False)
    anchor = spread(picked, "tm", root_device)
    return anchor[None] + prefix


def solution(mesh):
    placed = (P("tm", None, "gz", None, None), P(), P(), P(), P(), P(), P(), P())
    return jax.shard_map(
        shards,
        mesh=mesh,
        in_specs=placed,
        out_specs=P("tm", None, "gz", None, None),
        check_vma=False,
    )
```

profile of v0, /device:TPU:225, one launch (start us, length us, event | category | flops | bytes accessed | tf_op | source)
XLA Modules:
  0.0 656.7 jit_solution(2371562767231627077)
XLA Ops:
  8.9 4.0 collective-permute-start.1
  15.3 3.3 collective-permute-done
  19.9 213.8 %while.31 = (s32[]{:T(128)}, f32[4,4,128,128]{3,2,0,1:T(8,128)}, s32[4]{0:T(128)S(1)}, f32[4,6,128,128]{3,2,1,0:T(8,128)S(1)}, f32[32,108]{1,0:T(8,128)S(1)}, /*...) while((s32[]{:T(128)}, f32[4,4,128,128]{3,2,0,1:T(8,128)}, ...), condition=%wide.region_2.3_spmd, body=%wide.region_1.2_spmd.sunk | while | flops 709689344 | bytes 80493440 | solution.py:96
  41.8 22.0 %concatenate.159 = f32[108,16384]{1,0:T(8,128)} concatenate(f32[4,16384]{1,0:T(4,128)} %bitcast.325, f32[4,16384]{1,0:T(4,128)} %bitcast.323, f32[4,16384]{1,0:T(4,128)} %bitcast.322, f32[4,16384]{1,0:T(4,128)} %bitcast.320, f32[4,16384]{1,0:T(4,128)} %bitcast.326, f32[4,16384]{1,0:T(4,128)} %bitcast.321, f32[4,16384]{1,0:T(4,128)} %bitcast.318, f32[4,16384]{1,0:T(4,128)} %bitcast.324, ...), dimensions={0} | concatenate | bytes 14155776 | tf_op jit(solution)/shard_map/while/body/eval_jaxpr/while/body/eval_jaxpr/concatenate | solution.py:80
  63.8 7.2 %fusion.118 = f32[32,16384]{1,0:T(8,128)S(1)} fusion(f32[108,16384]{1,0:T(8,128)} %concatenate.159, f32[32,108]{1,0:T(8,128)S(1)} %get-tuple-element.488, f32[32]{0:T(128)S(1)} %get-tuple-element.489), kind=kOutput, calls=%fused_computation.1.clone.1 | convolution fusion | flops 680001536 | bytes 9188992 | tf_op jit(solution)/shard_map/while/body/eval_jaxpr/while/body/eval_jaxpr/dot_general | solution.py:81
  71.0 1.6 fusion.119
  95.2 22.0 %concatenate.159 = f32[108,16384]{1,0:T(8,128)} concatenate(f32[4,16384]{1,0:T(4,128)} %bitcast.325, f32[4,16384]{1,0:T(4,128)} %bitcast.323, f32[4,16384]{1,0:T(4,128)} %bitcast.322, f32[4,16384]{1,0:T(4,128)} %bitcast.320, f32[4,16384]{1,0:T(4,128)} %bitcast.326, f32[4,16384]{1,0:T(4,128)} %bitcast.321, f32[4,16384]{1,0:T(4,128)} %bitcast.318, f32[4,16384]{1,0:T(4,128)} %bitcast.324, ...), dimensions={0} | concatenate | bytes 14155776 | tf_op jit(solution)/shard_map/while/body/eval_jaxpr/while/body/eval_jaxpr/concatenate | solution.py:80
  117.3 7.2 %fusion.118 = f32[32,16384]{1,0:T(8,128)S(1)} fusion(f32[108,16384]{1,0:T(8,128)} %concatenate.159, f32[32,108]{1,0:T(8,128)S(1)} %get-tuple-element.488, f32[32]{0:T(128)S(1)} %get-tuple-element.489), kind=kOutput, calls=%fused_computation.1.clone.1 | convolution fusion | flops 680001536 | bytes 9188992 | tf_op jit(solution)/shard_map/while/body/eval_jaxpr/while/body/eval_jaxpr/dot_general | solution.py:81
  124.5 1.6 fusion.119
  148.7 22.0 %concatenate.159 = f32[108,16384]{1,0:T(8,128)} concatenate(f32[4,16384]{1,0:T(4,128)} %bitcast.325, f32[4,16384]{1,0:T(4,128)} %bitcast.323, f32[4,16384]{1,0:T(4,128)} %bitcast.322, f32[4,16384]{1,0:T(4,128)} %bitcast.320, f32[4,16384]{1,0:T(4,128)} %bitcast.326, f32[4,16384]{1,0:T(4,128)} %bitcast.321, f32[4,16384]{1,0:T(4,128)} %bitcast.318, f32[4,16384]{1,0:T(4,128)} %bitcast.324, ...), dimensions={0} | concatenate | bytes 14155776 | tf_op jit(solution)/shard_map/while/body/eval_jaxpr/while/body/eval_jaxpr/concatenate | solution.py:80
  170.7 7.2 %fusion.118 = f32[32,16384]{1,0:T(8,128)S(1)} fusion(f32[108,16384]{1,0:T(8,128)} %concatenate.159, f32[32,108]{1,0:T(8,128)S(1)} %get-tuple-element.488, f32[32]{0:T(128)S(1)} %get-tuple-element.489), kind=kOutput, calls=%fused_computation.1.clone.1 | convolution fusion | flops 680001536 | bytes 9188992 | tf_op jit(solution)/shard_map/while/body/eval_jaxpr/while/body/eval_jaxpr/dot_general | solution.py:81
  178.0 1.6 fusion.119
  202.2 22.0 %concatenate.159 = f32[108,16384]{1,0:T(8,128)} concatenate(f32[4,16384]{1,0:T(4,128)} %bitcast.325, f32[4,16384]{1,0:T(4,128)} %bitcast.323, f32[4,16384]{1,0:T(4,128)} %bitcast.322, f32[4,16384]{1,0:T(4,128)} %bitcast.320, f32[4,16384]{1,0:T(4,128)} %bitcast.326, f32[4,16384]{1,0:T(4,128)} %bitcast.321, f32[4,16384]{1,0:T(4,128)} %bitcast.318, f32[4,16384]{1,0:T(4,128)} %bitcast.324, ...), dimensions={0} | concatenate | bytes 14155776 | tf_op jit(solution)/shard_map/while/body/eval_jaxpr/while/body/eval_jaxpr/concatenate | solution.py:80
  224.2 7.2 %fusion.118 = f32[32,16384]{1,0:T(8,128)S(1)} fusion(f32[108,16384]{1,0:T(8,128)} %concatenate.159, f32[32,108]{1,0:T(8,128)S(1)} %get-tuple-element.488, f32[32]{0:T(128)S(1)} %get-tuple-element.489), kind=kOutput, calls=%fused_computation.1.clone.1 | convolution fusion | flops 680001536 | bytes 9188992 | tf_op jit(solution)/shard_map/while/body/eval_jaxpr/while/body/eval_jaxpr/dot_general | solution.py:81
  231.4 1.6 fusion.119
  235.6 184.5 %all-gather.3.cloned.1.call-done = f32[128,4,128,128]{3,2,1,0:T(8,128)} async-done(((f32[4,4,128,128]{3,2,1,0:T(8,128)}), f32[128,4,128,128]{3,2,1,0:T(8,128)}) %all-gather.3.cloned.1.call-update) | async-done | bytes 33554448 | tf_op jit(solution)/shard_map/all_gather | solution.py:25
  420.1 51.8 %while.32 = (s32[]{:T(128)}, f32[4,4,128,128]{3,2,1,0:T(8,128)S(1)}, s32[]{:T(128)}, f32[32,4,4,128,128]{4,3,2,1,0:T(8,128)}, s32[]{:T(128)}, /*index=5*/s32[]{:T(128)}) while((s32[]{:T(128)}, f32[4,4,128,128]{3,2,1,0:T(8,128)S(1)}, s32[]{:T(128)}, f32[32,4,4,128,128]{4,3,2,1,0:T(8,128)}, s32[]{:T(128)}, ...), condition=%wide.region_4.5_spmd.clone, body=%wide.region_3.4_spmd.clone.sunk | while | flops 786436 | bytes 3145821 | solution.py:33
  420.1 1.7 add_select_fusion.2
  438.0 1.6 add_select_fusion.2
  439.6 1.6 add_select_fusion.2
  444.5 1.6 add_select_fusion.2
  446.1 1.6 add_select_fusion.2
  471.9 175.5 %all-reduce.2.cloned.1.call-done = f32[4,4,128,128]{3,2,1,0:T(8,128)} async-done(((f32[4,4,128,128]{3,2,1,0:T(8,128)}), f32[4,4,128,128]{3,2,1,0:T(8,128)}) %all-reduce.2.cloned.1.call-update) | async-done | bytes 1048592 | tf_op jit(solution)/shard_map/psum | solution.py:38
  647.4 2.4 add_bitcast_fusion
  (342 shorter events, 130.9 us)
Async XLA Ops:
  6.5 7.9 %copy-start = (f32[64,32]{0,1:T(8,128)S(1)}, f32[64,32]{0,1:T(8,128)}, u32[]{:S(2)}) copy-start(f32[64,32]{0,1:T(8,128)} %param.16) | copy-start | bytes 24580
  6.5 13.4 %copy-start.5 = (f32[4,32]{1,0:T(4,128)S(1)}, f32[4,32]{1,0:T(4,128)}, u32[]{:S(2)}) copy-start(f32[4,32]{1,0:T(4,128)} %param.19) | copy-start | bytes 1540
  6.5 413.6 %all-gather.3.cloned.1.call-start = ((), (), s32[]{:S(2)}) async-start(), calls=%async_computation.1 | async-start | bytes 34603008 | tf_op jit(solution)/shard_map/all_gather | solution.py:25
  7.6 10.9 %collective-permute-start = (f32[1,4,1,128,128]{4,3,2,1,0:T(8,128)S(1)}, f32[1,4,1,128,128]{4,3,2,1,0:T(8,128)S(1)}, u32[]{:S(2)}, u32[]{:S(2)}) collective-permute-start(f32[1,4,1,128,128]{4,3,2,1,0:T(8,128)S(1)} %get-tuple-element.270), channel_id=1, source_target_pairs={{0,1},{1,2},{2,3},{3,4},{4,5},{5,6},{6,7},{7,0},{8,9},{9,10},{10,1... | collective-permute-start | bytes 786440 | tf_op jit(solution)/shard_map/ppermute | solution.py:15
  8.9 9.7 %collective-permute-start.1 = (f32[1,4,1,128,128]{4,3,2,1,0:T(8,128)S(1)}, f32[1,4,1,128,128]{4,3,2,1,0:T(8,128)S(1)}, u32[]{:S(2)}, u32[]{:S(2)}) collective-permute-start(f32[1,4,1,128,128]{4,3,2,1,0:T(8,128)S(1)} %get-tuple-element.271), channel_id=1, source_target_pairs={{1,0},{2,1},{3,2},{4,3},{5,4},{6,5},{7,6},{0,7},{9,8},{10,9},{11,1... | collective-permute-start | bytes 786440 | tf_op jit(solution)/shard_map/ppermute | solution.py:18
  19.9 2.9 copy-start.2
  71.0 2.4 copy-start.3
  73.4 2.9 copy-start.2
  124.5 2.4 copy-start.3
  126.9 2.9 copy-start.2
  178.0 2.4 copy-start.3
  180.3 2.9 copy-start.2
  231.4 2.4 copy-start.3
  233.8 413.7 %all-reduce.2.cloned.1.call-start = ((), (), s32[]{:S(2)}) async-start(), calls=%async_computation | async-start | bytes 2097152 | tf_op jit(solution)/shard_map/psum | solution.py:38
  420.1 227.3 %copy-start.4 = (f32[4,4,128,128]{3,2,0,1:T(8,128)S(1)}, f32[4,4,128,128]{3,2,0,1:T(8,128)}, u32[]{:S(2)}) copy-start(f32[4,4,128,128]{3,2,0,1:T(8,128)} %get-tuple-element.145) | copy-start | bytes 3145732
  647.4 2.4 copy-start.1
Sparse Core Ops, SparseCore 0:
  233.9 186.1 all-gather.2
  422.8 224.6 all-reduce.1
where the time goes:
time: 665 us; the launch traced here: 657 us
  waiting for transfers between devices  363 us (55%)
  local copies, waits for them, and re-layouts  155 us (23%)
  other arithmetic  72.2 us (11%)
  matrix products  36.1 us (5%)
  between operations  14.8 us (2%)
  loops' own time  9.96 us (1%)
    all_gather x1, waiting for transfers between devices, carried_in(): everything = lax.all_gather(shard, axis)  185 us
    psum x1, waiting for transfers between devices, spread(): return lax.psum(jnp.where(mine, shard, jnp.zeros_like(shard)), axis)  176 us
    concatenate x8, local copies, waits for them, and re-layouts, one_plane(): jnp.concatenate(pieces, axis=0).reshape(27 * channels, rows_y * cols_x)  92.5 us
    while x120, local copies, waits for them, and re-layouts  51.6 us
    select_n x32, other arithmetic, hop(): return jnp.where(reached, new, before)  51 us
    dot_general x4, matrix products, one_plane(): jnp.dot(stacked_weight, stacked, precision=lax.Precision.HIGHEST, preferr...  28.8 us
  transfers between devices with their start and end apart: 4, of which 3 were waited for; matrix products, arithmetic and copies ran while one was open for 8% of the time, Pallas kernels for 0%

commit v1 on v0

v1 whole, which is shorter than its diff:
```python
import functools

import jax
import jax.numpy as jnp
import numpy as np
from jax import lax
from jax.experimental import pallas as pl
from jax.experimental.pallas import tpu as pltpu
from jax.sharding import PartitionSpec as P

STEP_SIZE = 0.125
MESH = pl.DeviceIdType.MESH

BLOCK = 80
WINDOW = 3 * BLOCK
TILE = 8
PIECES = 4
EARLY = 4
F32, BF16 = jnp.float32, jnp.bfloat16


def selector(channels, planes):
    chosen = np.zeros((27, channels, planes, WINDOW), np.float32)
    for b in range(3):
        for e in range(3):
            for zo in range(planes):
                for a in range(3):
                    zi = zo + a - 1
                    for i in range(channels):
                        if zi < 0:
                            plane = channels * planes + i
                        elif zi >= planes:
                            plane = channels * planes + channels + i
                        else:
                            plane = i * planes + zi
                        chosen[9 * a + 3 * b + e, i, zo, BLOCK * b + 24 * e + plane] = 1.0
    return chosen


def split(value):
    high = value.astype(BF16)
    return high, (value - high.astype(F32)).astype(BF16)


def kernel(
    first_ref, state_hbm, weight_ref, mix_ref, out_ref,
    st, halo, patch_hi, patch_lo, weight_hl, mix_hl, inc,
    mine, pm, dr, ds, pv, ur, us, yr, ys, fs,
    local_sem, halo_send, halo_recv, pm_send, pm_recv, d_send, d_recv,
    e_send, e_recv, u_send, u_recv, y_send, y_recv, f_send, f_recv,
):
    planes16 = st.shape[0]
    channels, planes = state_hbm.shape[0], state_hbm.shape[1]
    half = st.shape[2]
    rows = 2 * half
    chunks = half // TILE
    t, g = lax.axis_index("tm"), lax.axis_index("gz")
    count = lax.axis_size("tm")
    levels = count // 4
    ring = lax.axis_size("gz")
    core = t % 2
    other = 1 - core
    side = (t // 2) % 2
    z = t // 4
    top = levels - 1
    partner = t + 1 - 2 * core
    across = t + 2 - 4 * side
    after, before = (g + 1) % ring, (g + ring - 1) % ring

    fetch = pltpu.make_async_copy(state_hbm, st.reshape(channels, planes, 2, half, 128), local_sem)
    fetch.start()

    barrier = pltpu.get_barrier_semaphore()
    pl.semaphore_signal(barrier, inc=1, device_id={"tm": partner}, device_id_type=MESH)
    pl.semaphore_signal(barrier, inc=1, device_id={"tm": across}, device_id_type=MESH)
    pl.semaphore_signal(barrier, inc=1, device_id={"gz": after}, device_id_type=MESH)
    pl.semaphore_signal(barrier, inc=1, device_id={"gz": before}, device_id_type=MESH)

    pl.semaphore_signal(barrier, inc=1, device_id={"tm": (t + 4) % count}, device_id_type=MESH)
    pl.semaphore_signal(barrier, inc=1, device_id={"tm": (t + count - 4) % count}, device_id_type=MESH)
    pl.semaphore_wait(barrier, 6)

    span = half // PIECES

    def halo_copies(piece):
        at = pl.ds(span * piece, span)
        up = pltpu.make_async_remote_copy(
            src_ref=state_hbm.at[:, planes - 1, :, at, :],
            dst_ref=halo.at[0:channels, :, at, :],
            send_sem=halo_send.at[0, piece], recv_sem=halo_recv.at[0, piece],
            device_id={"gz": after}, device_id_type=MESH,
        )
        down = pltpu.make_async_remote_copy(
            src_ref=state_hbm.at[:, 0, :, at, :],
            dst_ref=halo.at[channels : 2 * channels, :, at, :],
            send_sem=halo_send.at[1, piece], recv_sem=halo_recv.at[1, piece],
            device_id={"gz": before}, device_id_type=MESH,
        )
        return up, down

    halos = {}
    for piece in [PIECES - 1] + list(range(PIECES - 1)):
        halos[piece] = halo_copies(piece)
        for copy in halos[piece]:
            copy.start()

    fetch.wait()

    is_first = jnp.where(first_ref[0] == t, 1.0, 0.0).astype(F32)

    @pl.loop(0, planes16)
    def _(p):
        mine[p] = st[p] * is_first

    pm_copy = pltpu.make_async_remote_copy(
        src_ref=mine.at[:, other], dst_ref=pm, send_sem=pm_send, recv_sem=pm_recv,
        device_id={"tm": partner}, device_id_type=MESH,
    )
    pm_copy.start()

    high, low = split(weight_ref[...])
    wide = high.shape[0]
    weight_hl[0:wide] = high
    weight_hl[wide : 2 * wide] = low
    high, low = split(mix_ref[...])
    weight16 = high.shape[0]
    mix_hl[0:weight16] = high
    mix_hl[weight16 : 2 * weight16] = low

    st2 = st.reshape(planes16 * rows, 128)
    halo2 = halo.reshape(2 * channels * rows, 128)
    inc2 = inc.reshape(planes16 * rows, 128)
    ones = jnp.ones((8, 128), F32)

    def build(y):
        where = pl.multiple_of(BLOCK * (y + 1), 16)
        for lane, row in ((0, (y + rows) % rows), (128, (y + half) % rows)):
            body = jnp.concatenate(
                [st2[pl.ds(row, planes16, stride=rows), :], halo2[pl.ds(row, 2 * channels, stride=rows), :]], axis=0
            )
            full = jnp.concatenate([pltpu.roll(body, 1, 1), body, pltpu.roll(body, 127, 1), ones], axis=0)
            high, low = split(full)
            patch_hi[pl.ds(where, BLOCK), lane : lane + 128] = high
            patch_lo[pl.ds(where, BLOCK), lane : lane + 128] = low

    def drift(y):
        window = pl.ds(pl.multiple_of(BLOCK * y, 16), WINDOW)
        both = jnp.dot(weight_hl[...], patch_hi[window, :], preferred_element_type=F32)
        hidden = both[0:wide] + both[wide : 2 * wide] + jnp.dot(
            weight_hl[0:wide], patch_lo[window, :], preferred_element_type=F32
        )
        active = hidden + hidden * jnp.tanh(hidden)
        high, low = split(active)
        both = jnp.dot(mix_hl[...], high, preferred_element_type=F32)
        result = both[0:weight16] + both[weight16 : 2 * weight16] + jnp.dot(
            mix_hl[0:weight16], low, preferred_element_type=F32
        )
        inc2[pl.ds(y, planes16, stride=rows), :] = result[:, 0:128]
        inc2[pl.ds(y + half, planes16, stride=rows), :] = result[:, 128:256]

    def to(refs, j, sends, recvs, device):
        src, dst = refs
        return pltpu.make_async_remote_copy(
            src_ref=src, dst_ref=dst, send_sem=sends.at[j], recv_sem=recvs.at[j],
            device_id={"tm": device}, device_id_type=MESH,
        )

    def at(j):
        return pl.ds(pl.multiple_of(TILE * j, TILE), TILE)

    def e_copy(j):
        return to((inc.at[:, other, at(j), :], pv.at[:, at(j), :]), j, e_send, e_recv, partner)

    def d_copy(j):
        return to((ds.at[:, at(j), :], dr.at[:, at(j), :]), j, d_send, d_recv, t - 4)

    def u_copy(j):
        return to((us.at[:, at(j), :], ur.at[:, at(j), :]), j, u_send, u_recv, t + 4)

    def y_copy(j):
        return to((ys.at[:, at(j), :], yr.at[:, at(j), :]), j, y_send, y_recv, across)

    def f_copy(j):
        return to((fs.at[:, at(j), :], out_ref.at[:, core, at(j), :]), j, f_send, f_recv, partner)

    pm_copy.wait()

    d_slot = 2 * (top - z)
    u_slot = 2 * z + 1 + EARLY
    y_slot = jnp.maximum(u_slot, d_slot + 1)
    f_slot = y_slot + 2
    need = {0: [PIECES - 1, 0]}
    for piece in range(1, PIECES):
        if piece < PIECES - 1:
            need[span * piece // TILE - 1] = [piece]

    def turn(n, _):
        k = n - EARLY
        for chunk, pieces in need.items():
            @pl.when(k == chunk)
            def _():
                for piece in pieces:
                    for copy in halos[piece]:
                        copy.wait_recv()

        @pl.when(k == 0)
        def _():
            build(-1)
            build(0)

        @pl.when((k >= 0) & (k < chunks))
        def _():
            first = TILE * k

            @pl.loop(0, TILE // 2)
            def _(n):
                build(first + 2 * n + 1)
                build(first + 2 * n + 2)

            @pl.loop(0, TILE // 2)
            def _(n):
                drift(first + 2 * n)
                drift(first + 2 * n + 1)

            e_copy(k).start()

        jd = n - d_slot

        @pl.when((jd >= 0) & (jd < chunks))
        def _():
            rows_j = at(jd)

            @pl.when(z < top)
            def _():
                d_copy(jd).wait_recv()

            @pl.when(z == top)
            def _():
                dr[:, rows_j, :] = jnp.zeros((planes16, TILE, 128), F32)

            @pl.when(z > 0)
            def _():
                ds[:, rows_j, :] = dr[:, rows_j, :] + mine[:, core, rows_j, :] + pm[:, rows_j, :]
                d_copy(jd).start()

        ju = n - u_slot

        @pl.when((ju >= 0) & (ju < chunks))
        def _():
            rows_j = at(ju)
            e_copy(ju).wait_recv()

            @pl.when(z > 0)
            def _():
                u_copy(ju).wait_recv()

            @pl.when(z == 0)
            def _():
                ur[:, rows_j, :] = jnp.zeros((planes16, TILE, 128), F32)

            @pl.when(z < top)
            def _():
                us[:, rows_j, :] = (
                    ur[:, rows_j, :] + inc[:, core, rows_j, :] + pv[:, rows_j, :]
                    + mine[:, core, rows_j, :] + pm[:, rows_j, :]
                )
                u_copy(ju).start()

        jy = n - y_slot

        @pl.when((jy >= 0) & (jy < chunks))
        def _():
            rows_j = at(jy)
            total = ur[:, rows_j, :] + dr[:, rows_j, :] + mine[:, core, rows_j, :] + pm[:, rows_j, :]
            own = inc[:, core, rows_j, :] + pv[:, rows_j, :]
            ys[:, rows_j, :] = jnp.where(side == 0, total + own, total)
            y_copy(jy).start()

        jf = n - f_slot

        @pl.when((jf >= 0) & (jf < chunks))
        def _():
            rows_j = at(jf)
            y_copy(jf).wait_recv()
            total = (
                ur[:, rows_j, :] + dr[:, rows_j, :] + mine[:, core, rows_j, :] + pm[:, rows_j, :] + yr[:, rows_j, :]
            )
            out_ref[:, core, rows_j, :] = jnp.where(core == 1, total + pv[:, rows_j, :], total)
            fs[:, rows_j, :] = jnp.where(core == 0, total + inc[:, core, rows_j, :], total)
            f_copy(jf).start()

        return 0

    lax.fori_loop(0, chunks + 2 * top + 3 + EARLY, turn, 0)

    for pair in halos.values():
        for copy in pair:
            copy.wait_send()

    @pl.loop(0, chunks)
    def _(j):
        e_copy(j).wait_send()
        y_copy(j).wait_send()
        f_copy(j).wait()

        @pl.when(z > 0)
        def _():
            d_copy(j).wait_send()

        @pl.when(z < top)
        def _():
            u_copy(j).wait_send()


def shards(
    states, first_unconverged, window_offset, summaries, cond_weight, time_gain, conv_weight, out_weight
):
    channels, planes, rows, cols = states.shape[1:]
    hidden = conv_weight.shape[1]
    half = rows // 2
    steps = states.shape[0] * lax.axis_size("tm")
    step = lax.axis_index("tm")
    step_time = 1.0 - (window_offset[0] + step).astype(F32) / float(steps + 64)
    condition = jnp.dot(summaries, cond_weight, precision=lax.Precision.HIGHEST, preferred_element_type=F32)
    offset = condition + step_time * time_gain
    chosen = selector(channels, planes)
    weight = jnp.einsum("oci,oizk->zck", conv_weight, chosen, precision=lax.Precision.HIGHEST)
    marker = np.zeros((WINDOW,), np.float32)
    marker[72] = 1.0
    weight = 0.5 * (weight + offset[None, :, None] * marker).reshape(planes * hidden, WINDOW)
    mix = STEP_SIZE * jnp.einsum("ic,zw->izwc", out_weight, np.eye(planes, dtype=np.float32), precision=lax.Precision.HIGHEST)
    mix = mix.reshape(channels * planes, planes * hidden)
    state = states.reshape(channels, planes, 2, half, cols)
    p16 = channels * planes
    chunks = half // TILE
    half_shape = pltpu.VMEM((p16, half, cols), F32)
    whole_shape = pltpu.VMEM((p16, 2, half, cols), F32)
    dma = pltpu.SemaphoreType.DMA
    out = pl.pallas_call(
        kernel,
        name="picard",
        out_shape=jax.ShapeDtypeStruct((p16, 2, half, cols), F32),
        in_specs=[
            pl.BlockSpec(memory_space=pltpu.SMEM),
            pl.BlockSpec(memory_space=pl.ANY),
            pl.BlockSpec(memory_space=pltpu.VMEM),
            pl.BlockSpec(memory_space=pltpu.VMEM),
        ],
        out_specs=pl.BlockSpec(memory_space=pltpu.VMEM),
        scratch_shapes=[
            whole_shape,
            pltpu.VMEM((2 * channels, 2, half, cols), F32),
            pltpu.VMEM(((half + 2) * BLOCK, 256), BF16),
            pltpu.VMEM(((half + 2) * BLOCK, 256), BF16),
            pltpu.VMEM((2 * planes * hidden, WINDOW), BF16),
            pltpu.VMEM((2 * p16, planes * hidden), BF16),
            whole_shape,
            whole_shape,
        ]
        + [half_shape] * 9
        + [dma, dma((2, PIECES)), dma((2, PIECES)), dma, dma]
        + [dma((chunks,))] * 10,
        compiler_params=pltpu.CompilerParams(
            collective_id=0, has_side_effects=True, vmem_limit_bytes=48 * 1024 * 1024
        ),
    )(first_unconverged, state, weight, mix)
    return out.reshape(states.shape)


def solution(mesh):
    placed = (P("tm", None, "gz", None, None), P(), P(), P(), P(), P(), P(), P())
    return jax.shard_map(
        shards,
        mesh=mesh,
        in_specs=placed,
        out_specs=P("tm", None, "gz", None, None),
        check_vma=False,
    )
```

time: 665 us -> 76.4 us (0.11); the launches traced: 657 us -> 76.2 us
  waiting for transfers between devices: 363 us -> 0 us
  local copies, waits for them, and re-layouts: 155 us -> 3.51 us
  other arithmetic: 72.2 us -> 0.15 us
  Pallas kernels: 0 us -> 69.5 us
  matrix products: 36.1 us -> 1.61 us
  between operations: 14.8 us -> 1.41 us
  loops' own time: 9.96 us -> 0 us
    all_gather x1 -> x0, waiting for transfers between devices: 185 us -> none  [carried_in(): everything = lax.all_gather(shard, axis)]
    psum x1 -> x0, waiting for transfers between devices: 176 us -> none  [spread(): return lax.psum(jnp.where(mine, shard, jnp.zeros_like(shard)), axis)]
    concatenate x8 -> x0, local copies, waits for them, and re-layouts: 92.5 us -> none  [one_plane(): jnp.concatenate(pieces, axis=0).reshape(27 * channels, rows_y * cols_x)]
    pallas_call x0 -> x1, Pallas kernels: none -> 69.5 us  [shards(): pl.pallas_call(kernel, name='picard', out_shape=jax.ShapeDtypeStruct((p16...]
    select_n x33 -> x0, other arithmetic: 52.1 us -> none  [the longest x32 51 us: hop(): return jnp.where(reached, new, before)]
    while x121 -> x0, local copies, waits for them, and re-layouts: 51.7 us -> none
    dot_general x8 -> x1, matrix products: 35.3 us -> 1.49 us  [shards(): jnp.einsum('oci,oizk->zck', conv_weight, chosen, precision=lax.Precision....]
    while x88 -> x0, other arithmetic: 10.1 us -> none
  transfers between devices with their start and end apart: 4 -> 0, of which waited for: 3 -> 0; matrix products, arithmetic and copies ran while one was open for 8% -> 0% of each run, Pallas kernels for 0% -> 0%
where the time goes in v1:
time: 76.4 us; the launch traced here: 76.2 us
  Pallas kernels  69.5 us (91%)
  local copies, waits for them, and re-layouts  3.51 us (5%)
  matrix products  1.61 us (2%)
  between operations  1.41 us (2%)
    pallas_call x1, Pallas kernels, shards(): pl.pallas_call(kernel, name='picard', out_shape=jax.ShapeDtypeStruct((p16...  69.5 us
    unnamed x18, local copies, waits for them, and re-layouts  3.42 us

profile of v1, /device:TPU:225, one launch (start us, length us, event | category | flops | bytes accessed | tf_op | source)
XLA Modules:
  0.0 76.2 jit_solution(13226066473829798085)
XLA Ops:
  0.0 0.0 copy-start
  0.7 0.0 copy-start.6
  0.7 0.0 copy-start.7
  1.4 0.0 copy-done
  1.4 0.0 copy-done.6
  1.4 0.0 copy-done.7
  1.4 0.0 copy-start.5
  1.4 0.1 fusion.2
  1.5 0.0 copy-start.3
  1.5 0.0 copy-start.4
  1.5 0.5 copy-done.5
  2.1 0.0 copy-start.2
  2.1 0.1 broadcast_multiply_fusion
  2.1 0.1 copy-done.3
  2.2 0.0 copy-done.4
  2.2 0.1 multiply_bitcast_fusion
  2.3 0.1 reshape.45.mix_ref
  2.4 0.5 copy-done.2
  2.9 0.1 copy.12
  3.0 1.5 %fusion.1 = f32[4,32,240]{2,1,0:T(8,128)S(1)} fusion(f32[27,4,4,240]{3,0,1,2:T(8,128)} %constant.21.clone, f32[27,32,4]{0,1,2:T(8,128)S(1)} %copy.12, f32[32,240]{1,0:T(8,128)S(1)} %broadcast_multiply_fusion), kind=kOutput, calls=%fused_computation.2 | convolution fusion | flops 39874560 | bytes 582144 | tf_op jit(solution)/shard_map/oci,oizk->zck/dot_general | solution.py:327
  4.5 0.0 copy-start.1
  4.5 1.2 %copy-done.1 = f32[1,4,4,128,128]{4,3,2,1,0:T(8,128)S(1)} copy-done((f32[1,4,4,128,128]{4,3,2,1,0:T(8,128)S(1)}, f32[1,4,4,128,128]{4,3,2,1,0:T(8,128)}, u32[]{:S(2)}) %copy-start.1) | copy-done | bytes 1048600
  5.7 69.5 %picard.1 = f32[16,2,64,128]{3,2,1,0:T(8,128)S(1)} custom-call(s32[1]{0:T(128)S(6)} %copy.15.first_ref, f32[4,4,2,64,128]{4,3,2,1,0:T(8,128)S(1)} %bitcast.29, f32[128,240]{1,0:T(8,128)S(1)} %bitcast.30, f32[16,128]{1,0:T(8,128)S(1)} %reshape.45.mix_ref), custom_call_target="tpu_custom_call" | custom-call | tf_op jit(solution)/shard_map/picard/pallas_call | solution.py:339
  75.2 1.0 %copy.17 = f32[1,4,4,128,128]{4,3,2,1,0:T(8,128)} copy(f32[1,4,4,128,128]{4,3,2,1,0:T(8,128)S(1)} %bitcast.28) | data formatting | bytes 2097152
Async XLA Ops:
  0.0 1.4 %copy-start = (f32[64,32]{0,1:T(8,128)S(1)}, f32[64,32]{0,1:T(8,128)}, u32[]{:S(2)}) copy-start(f32[64,32]{0,1:T(8,128)} %param.15) | copy-start | bytes 24580
  0.7 0.7 copy-start.6
  0.7 0.7 copy-start.7
  1.4 0.7 copy-start.5
  1.5 0.7 copy-start.3
  1.5 0.7 copy-start.4
  2.1 0.8 %copy-start.2 = (f32[27,32,4]{1,2,0:T(4,128)S(1)}, f32[27,32,4]{1,2,0:T(4,128)}, u32[]{:S(2)}) copy-start(f32[27,32,4]{1,2,0:T(4,128)} %param.17) | copy-start | bytes 41476
  4.5 1.2 %copy-start.1 = (f32[1,4,4,128,128]{4,3,2,1,0:T(8,128)S(1)}, f32[1,4,4,128,128]{4,3,2,1,0:T(8,128)}, u32[]{:S(2)}) copy-start(f32[1,4,4,128,128]{4,3,2,1,0:T(8,128)} %param.11) | copy-start | bytes 3145732

commit v2 on v1

--- a/solution.py
+++ b/solution.py
@@ -16,6 +16,7 @@
 TILE = 8
 PIECES = 4
 EARLY = 4
+PARTS = 2
 F32, BF16 = jnp.float32, jnp.bfloat16
 
 
@@ -158,30 +159,33 @@
         inc2[pl.ds(y, planes16, stride=rows), :] = result[:, 0:128]
         inc2[pl.ds(y + half, planes16, stride=rows), :] = result[:, 128:256]
 
-    def to(refs, j, sends, recvs, device):
+    def to(refs, j, part, sends, recvs, device):
         src, dst = refs
         return pltpu.make_async_remote_copy(
-            src_ref=src, dst_ref=dst, send_sem=sends.at[j], recv_sem=recvs.at[j],
+            src_ref=src, dst_ref=dst, send_sem=sends.at[j, part], recv_sem=recvs.at[j, part],
             device_id={"tm": device}, device_id_type=MESH,
         )
+
+    share = planes16 // PARTS
+    parts = [(part, slice(share * part, share * (part + 1))) for part in range(PARTS)]
 
     def at(j):
         return pl.ds(pl.multiple_of(TILE * j, TILE), TILE)
 
-    def e_copy(j):
-        return to((inc.at[:, other, at(j), :], pv.at[:, at(j), :]), j, e_send, e_recv, partner)
-
-    def d_copy(j):
-        return to((ds.at[:, at(j), :], dr.at[:, at(j), :]), j, d_send, d_recv, t - 4)
-
-    def u_copy(j):
-        return to((us.at[:, at(j), :], ur.at[:, at(j), :]), j, u_send, u_recv, t + 4)
-
-    def y_copy(j):
-        return to((ys.at[:, at(j), :], yr.at[:, at(j), :]), j, y_send, y_recv, across)
-
-    def f_copy(j):
-        return to((fs.at[:, at(j), :], out_ref.at[:, core, at(j), :]), j, f_send, f_recv, partner)
+    def e_copy(j, part, w):
+        return to((inc.at[w, other, at(j), :], pv.at[w, at(j), :]), j, part, e_send, e_recv, partner)
+
+    def d_copy(j, part, w):
+        return to((ds.at[w, at(j), :], dr.at[w, at(j), :]), j, part, d_send, d_recv, t - 4)
+
+    def u_copy(j, part, w):
+        return to((us.at[w, at(j), :], ur.at[w, at(j), :]), j, part, u_send, u_recv, t + 4)
+
+    def y_copy(j, part, w):
+        return to((ys.at[w, at(j), :], yr.at[w, at(j), :]), j, part, y_send, y_recv, across)
+
+    def f_copy(j, part, w):
+        return to((fs.at[w, at(j), :], out_ref.at[w, core, at(j), :]), j, part, f_send, f_recv, partner)
 
     pm_copy.wait()
 
@@ -222,72 +226,77 @@
                 drift(first + 2 * n)
                 drift(first + 2 * n + 1)
 
-            e_copy(k).start()
+            for part, w in parts:
+                e_copy(k, part, w).start()
 
         jd = n - d_slot
 
         @pl.when((jd >= 0) & (jd < chunks))
         def _():
             rows_j = at(jd)
-
-            @pl.when(z < top)
-            def _():
-                d_copy(jd).wait_recv()
-
-            @pl.when(z == top)
-            def _():
-                dr[:, rows_j, :] = jnp.zeros((planes16, TILE, 128), F32)
-
-            @pl.when(z > 0)
-            def _():
-                ds[:, rows_j, :] = dr[:, rows_j, :] + mine[:, core, rows_j, :] + pm[:, rows_j, :]
-                d_copy(jd).start()
+            for part, w in parts:
+                @pl.when(z < top)
+                def _():
+                    d_copy(jd, part, w).wait_recv()
+
+                @pl.when(z == top)
+                def _():
+                    dr[w, rows_j, :] = jnp.zeros((share, TILE, 128), F32)
+
+                @pl.when(z > 0)
+                def _():
+                    ds[w, rows_j, :] = dr[w, rows_j, :] + mine[w, core, rows_j, :] + pm[w, rows_j, :]
+                    d_copy(jd, part, w).start()
 
         ju = n - u_slot
 
         @pl.when((ju >= 0) & (ju < chunks))
         def _():
             rows_j = at(ju)
-            e_copy(ju).wait_recv()
-
-            @pl.when(z > 0)
-            def _():
-                u_copy(ju).wait_recv()
-
-            @pl.when(z == 0)
-            def _():
-                ur[:, rows_j, :] = jnp.zeros((planes16, TILE, 128), F32)
-
-            @pl.when(z < top)
-            def _():
-                us[:, rows_j, :] = (
-                    ur[:, rows_j, :] + inc[:, core, rows_j, :] + pv[:, rows_j, :]
-                    + mine[:, core, rows_j, :] + pm[:, rows_j, :]
+            for part, w in parts:
+                e_copy(ju, part, w).wait_recv()
+
+                @pl.when(z > 0)
+                def _():
+                    u_copy(ju, part, w).wait_recv()
+
+                @pl.when(z == 0)
+                def _():
+                    ur[w, rows_j, :] = jnp.zeros((share, TILE, 128), F32)
+
+                @pl.when(z < top)
+                def _():
+                    us[w, rows_j, :] = (
+                        ur[w, rows_j, :] + inc[w, core, rows_j, :] + pv[w, rows_j, :]
+                        + mine[w, core, rows_j, :] + pm[w, rows_j, :]
+                    )
+                    u_copy(ju, part, w).start()
+
+        jy = n - y_slot
+
+        @pl.when((jy >= 0) & (jy < chunks))
+        def _():
+            rows_j = at(jy)
+            for part, w in parts:
+                total = ur[w, rows_j, :] + dr[w, rows_j, :] + mine[w, core, rows_j, :] + pm[w, rows_j, :]
+                own = inc[w, core, rows_j, :] + pv[w, rows_j, :]
+                ys[w, rows_j, :] = jnp.where(side == 0, total + own, total)
+                y_copy(jy, part, w).start()
+
+        jf = n - f_slot
+
+        @pl.when((jf >= 0) & (jf < chunks))
+        def _():
+            rows_j = at(jf)
+            for part, w in parts:
+                y_copy(jf, part, w).wait_recv()
+                total = (
+                    ur[w, rows_j, :] + dr[w, rows_j, :] + mine[w, core, rows_j, :] + pm[w, rows_j, :]
+                    + yr[w, rows_j, :]
                 )
-                u_copy(ju).start()
-
-        jy = n - y_slot
-
-        @pl.when((jy >= 0) & (jy < chunks))
-        def _():
-            rows_j = at(jy)
-            total = ur[:, rows_j, :] + dr[:, rows_j, :] + mine[:, core, rows_j, :] + pm[:, rows_j, :]
-            own = inc[:, core, rows_j, :] + pv[:, rows_j, :]
-            ys[:, rows_j, :] = jnp.where(side == 0, total + own, total)
-            y_copy(jy).start()
-
-        jf = n - f_slot
-
-        @pl.when((jf >= 0) & (jf < chunks))
-        def _():
-            rows_j = at(jf)
-            y_copy(jf).wait_recv()
-            total = (
-                ur[:, rows_j, :] + dr[:, rows_j, :] + mine[:, core, rows_j, :] + pm[:, rows_j, :] + yr[:, rows_j, :]
-            )
-            out_ref[:, core, rows_j, :] = jnp.where(core == 1, total + pv[:, rows_j, :], total)
-            fs[:, rows_j, :] = jnp.where(core == 0, total + inc[:, core, rows_j, :], total)
-            f_copy(jf).start()
+                out_ref[w, core, rows_j, :] = jnp.where(core == 1, total + pv[w, rows_j, :], total)
+                fs[w, rows_j, :] = jnp.where(core == 0, total + inc[w, core, rows_j, :], total)
+                f_copy(jf, part, w).start()
 
         return 0
 
@@ -299,17 +308,18 @@
 
     @pl.loop(0, chunks)
     def _(j):
-        e_copy(j).wait_send()
-        y_copy(j).wait_send()
-        f_copy(j).wait()
-
-        @pl.when(z > 0)
-        def _():
-            d_copy(j).wait_send()
-
-        @pl.when(z < top)
-        def _():
-            u_copy(j).wait_send()
+        for part, w in parts:
+            e_copy(j, part, w).wait_send()
+            y_copy(j, part, w).wait_send()
+            f_copy(j, part, w).wait()
+
+            @pl.when(z > 0)
+            def _():
+                d_copy(j, part, w).wait_send()
+
+            @pl.when(z < top)
+            def _():
+                u_copy(j, part, w).wait_send()
 
 
 def shards(
@@ -359,7 +369,7 @@
         ]
         + [half_shape] * 9
         + [dma, dma((2, PIECES)), dma((2, PIECES)), dma, dma]
-        + [dma((chunks,))] * 10,
+        + [dma((chunks, PARTS))] * 10,
         compiler_params=pltpu.CompilerParams(
             collective_id=0, has_side_effects=True, vmem_limit_bytes=48 * 1024 * 1024
         ),

time: 76.4 us -> 75.6 us (0.990)
  Pallas kernels: 69.5 us -> 68.7 us
    pallas_call x1, Pallas kernels: 69.5 us -> 68.7 us  [shards(): pl.pallas_call(kernel, name='picard', out_shape=jax.ShapeDtypeStruct((p16...]
where the time goes in v2:
time: 75.6 us; the launch traced here: 75.3 us
  Pallas kernels  68.7 us (91%)
  local copies, waits for them, and re-layouts  3.51 us (5%)
  matrix products  1.61 us (2%)
  between operations  1.41 us (2%)
    pallas_call x1, Pallas kernels, shards(): pl.pallas_call(kernel, name='picard', out_shape=jax.ShapeDtypeStruct((p16...  68.7 us
    unnamed x18, local copies, waits for them, and re-layouts  3.42 us

profile of v2, /device:TPU:225, one launch (start us, length us, event | category | flops | bytes accessed | tf_op | source)
XLA Modules:
  0.0 75.3 jit_solution(13853512635172524377)
XLA Ops:
  0.0 0.0 copy-start
  0.7 0.0 copy-start.6
  0.7 0.0 copy-start.7
  1.4 0.0 copy-done
  1.4 0.0 copy-done.6
  1.4 0.0 copy-done.7
  1.4 0.0 copy-start.5
  1.4 0.1 fusion.2
  1.5 0.0 copy-start.3
  1.5 0.0 copy-start.4
  1.5 0.5 copy-done.5
  2.1 0.0 copy-start.2
  2.1 0.1 broadcast_multiply_fusion
  2.1 0.1 copy-done.3
  2.2 0.0 copy-done.4
  2.2 0.1 multiply_bitcast_fusion
  2.3 0.1 reshape.45.mix_ref
  2.4 0.5 copy-done.2
  2.9 0.1 copy.12
  3.0 1.5 %fusion.1 = f32[4,32,240]{2,1,0:T(8,128)S(1)} fusion(f32[27,4,4,240]{3,0,1,2:T(8,128)} %constant.21.clone, f32[27,32,4]{0,1,2:T(8,128)S(1)} %copy.12, f32[32,240]{1,0:T(8,128)S(1)} %broadcast_multiply_fusion), kind=kOutput, calls=%fused_computation.2 | convolution fusion | flops 39874560 | bytes 582144 | tf_op jit(solution)/shard_map/oci,oizk->zck/dot_general | solution.py:337
  4.5 0.0 copy-start.1
  4.5 1.2 %copy-done.1 = f32[1,4,4,128,128]{4,3,2,1,0:T(8,128)S(1)} copy-done((f32[1,4,4,128,128]{4,3,2,1,0:T(8,128)S(1)}, f32[1,4,4,128,128]{4,3,2,1,0:T(8,128)}, u32[]{:S(2)}) %copy-start.1) | copy-done | bytes 1048600
  5.7 68.7 %picard.1 = f32[16,2,64,128]{3,2,1,0:T(8,128)S(1)} custom-call(s32[1]{0:T(128)S(6)} %copy.15.first_ref, f32[4,4,2,64,128]{4,3,2,1,0:T(8,128)S(1)} %bitcast.29, f32[128,240]{1,0:T(8,128)S(1)} %bitcast.30, f32[16,128]{1,0:T(8,128)S(1)} %reshape.45.mix_ref), custom_call_target="tpu_custom_call" | custom-call | tf_op jit(solution)/shard_map/picard/pallas_call | solution.py:349
  74.4 1.0 %copy.17 = f32[1,4,4,128,128]{4,3,2,1,0:T(8,128)} copy(f32[1,4,4,128,128]{4,3,2,1,0:T(8,128)S(1)} %bitcast.28) | data formatting | bytes 2097152
Async XLA Ops:
  0.0 1.4 %copy-start = (f32[64,32]{0,1:T(8,128)S(1)}, f32[64,32]{0,1:T(8,128)}, u32[]{:S(2)}) copy-start(f32[64,32]{0,1:T(8,128)} %param.15) | copy-start | bytes 24580
  0.7 0.7 copy-start.6
  0.7 0.7 copy-start.7
  1.4 0.7 copy-start.5
  1.5 0.7 copy-start.3
  1.5 0.7 copy-start.4
  2.1 0.8 %copy-start.2 = (f32[27,32,4]{1,2,0:T(4,128)S(1)}, f32[27,32,4]{1,2,0:T(4,128)}, u32[]{:S(2)}) copy-start(f32[27,32,4]{1,2,0:T(4,128)} %param.17) | copy-start | bytes 41476
  4.5 1.2 %copy-start.1 = (f32[1,4,4,128,128]{4,3,2,1,0:T(8,128)S(1)}, f32[1,4,4,128,128]{4,3,2,1,0:T(8,128)}, u32[]{:S(2)}) copy-start(f32[1,4,4,128,128]{4,3,2,1,0:T(8,128)} %param.11) | copy-start | bytes 3145732

commit v3 on v2

--- a/solution.py
+++ b/solution.py
@@ -14,7 +14,7 @@
 BLOCK = 80
 WINDOW = 3 * BLOCK
 TILE = 8
-PIECES = 4
+PIECES = 8
 EARLY = 4
 PARTS = 2
 F32, BF16 = jnp.float32, jnp.bfloat16
@@ -196,7 +196,7 @@
     need = {0: [PIECES - 1, 0]}
     for piece in range(1, PIECES):
         if piece < PIECES - 1:
-            need[span * piece // TILE - 1] = [piece]
+            need.setdefault(span * piece // TILE - 1, []).append(piece)
 
     def turn(n, _):
         k = n - EARLY
@@ -209,22 +209,19 @@
 
         @pl.when(k == 0)
         def _():
-            build(-1)
-            build(0)
+            for y in range(-1, 3):
+                build(y)
 
         @pl.when((k >= 0) & (k < chunks))
         def _():
             first = TILE * k
-
-            @pl.loop(0, TILE // 2)
-            def _(n):
-                build(first + 2 * n + 1)
-                build(first + 2 * n + 2)
 
             @pl.loop(0, TILE // 2)
             def _(n):
                 drift(first + 2 * n)
                 drift(first + 2 * n + 1)
+                build(first + 2 * n + 3)
+                build(first + 2 * n + 4)
 
             for part, w in parts:
                 e_copy(k, part, w).start()
@@ -360,8 +357,8 @@
         scratch_shapes=[
             whole_shape,
             pltpu.VMEM((2 * channels, 2, half, cols), F32),
-            pltpu.VMEM(((half + 2) * BLOCK, 256), BF16),
-            pltpu.VMEM(((half + 2) * BLOCK, 256), BF16),
+            pltpu.VMEM(((half + 4) * BLOCK, 256), BF16),
+            pltpu.VMEM(((half + 4) * BLOCK, 256), BF16),
             pltpu.VMEM((2 * planes * hidden, WINDOW), BF16),
             pltpu.VMEM((2 * p16, planes * hidden), BF16),
             whole_shape,

time: 75.6 us -> 71.9 us (0.951)
  Pallas kernels: 68.7 us -> 64.9 us
    pallas_call x1, Pallas kernels: 68.7 us -> 64.9 us  [shards(): pl.pallas_call(kernel, name='picard', out_shape=jax.ShapeDtypeStruct((p16...]
where the time goes in v3:
time: 71.9 us; the launch traced here: 71.6 us
  Pallas kernels  64.9 us (90%)
  local copies, waits for them, and re-layouts  3.51 us (5%)
  matrix products  1.61 us (2%)
  between operations  1.41 us (2%)
    pallas_call x1, Pallas kernels, shards(): pl.pallas_call(kernel, name='picard', out_shape=jax.ShapeDtypeStruct((p16...  64.9 us
    unnamed x18, local copies, waits for them, and re-layouts  3.42 us
    dot_general x1, matrix products, shards(): jnp.einsum('oci,oizk->zck', conv_weight, chosen, precision=lax.Precision....  1.49 us

profile of v3, /device:TPU:225, one launch (start us, length us, event | category | flops | bytes accessed | tf_op | source)
XLA Modules:
  0.0 71.6 jit_solution(221584765098150550)
XLA Ops:
  0.0 0.0 copy-start
  0.7 0.0 copy-start.6
  0.7 0.0 copy-start.7
  1.4 0.0 copy-done
  1.4 0.0 copy-done.6
  1.4 0.0 copy-done.7
  1.4 0.0 copy-start.5
  1.4 0.1 fusion.2
  1.5 0.0 copy-start.3
  1.5 0.0 copy-start.4
  1.5 0.5 copy-done.5
  2.1 0.0 copy-start.2
  2.1 0.1 broadcast_multiply_fusion
  2.1 0.1 copy-done.3
  2.2 0.0 copy-done.4
  2.2 0.1 multiply_bitcast_fusion
  2.3 0.1 reshape.45.mix_ref
  2.4 0.5 copy-done.2
  2.9 0.1 copy.12
  3.0 1.5 %fusion.1 = f32[4,32,240]{2,1,0:T(8,128)S(1)} fusion(f32[27,4,4,240]{3,0,1,2:T(8,128)} %constant.21.clone, f32[27,32,4]{0,1,2:T(8,128)S(1)} %copy.12, f32[32,240]{1,0:T(8,128)S(1)} %broadcast_multiply_fusion), kind=kOutput, calls=%fused_computation.2 | convolution fusion | flops 39874560 | bytes 582144 | tf_op jit(solution)/shard_map/oci,oizk->zck/dot_general | solution.py:334
  4.5 0.0 copy-start.1
  4.5 1.2 %copy-done.1 = f32[1,4,4,128,128]{4,3,2,1,0:T(8,128)S(1)} copy-done((f32[1,4,4,128,128]{4,3,2,1,0:T(8,128)S(1)}, f32[1,4,4,128,128]{4,3,2,1,0:T(8,128)}, u32[]{:S(2)}) %copy-start.1) | copy-done | bytes 1048600
  5.7 64.9 %picard.1 = f32[16,2,64,128]{3,2,1,0:T(8,128)S(1)} custom-call(s32[1]{0:T(128)S(6)} %copy.15.first_ref, f32[4,4,2,64,128]{4,3,2,1,0:T(8,128)S(1)} %bitcast.29, f32[128,240]{1,0:T(8,128)S(1)} %bitcast.30, f32[16,128]{1,0:T(8,128)S(1)} %reshape.45.mix_ref), custom_call_target="tpu_custom_call" | custom-call | tf_op jit(solution)/shard_map/picard/pallas_call | solution.py:346
  70.6 1.0 %copy.17 = f32[1,4,4,128,128]{4,3,2,1,0:T(8,128)} copy(f32[1,4,4,128,128]{4,3,2,1,0:T(8,128)S(1)} %bitcast.28) | data formatting | bytes 2097152
Async XLA Ops:
  0.0 1.4 %copy-start = (f32[64,32]{0,1:T(8,128)S(1)}, f32[64,32]{0,1:T(8,128)}, u32[]{:S(2)}) copy-start(f32[64,32]{0,1:T(8,128)} %param.15) | copy-start | bytes 24580
  0.7 0.7 copy-start.6
  0.7 0.7 copy-start.7
  1.4 0.7 copy-start.5
  1.5 0.7 copy-start.3
  1.5 0.7 %copy-start.4 = (f32[4,4]{1,0:T(4,128)S(1)}, f32[4,4]{1,0:T(4,128)}, u32[]{:S(2)}) copy-start(f32[4,4]{1,0:T(4,128)} %constant.23.clone) | copy-start | bytes 196
  2.1 0.8 %copy-start.2 = (f32[27,32,4]{1,2,0:T(4,128)S(1)}, f32[27,32,4]{1,2,0:T(4,128)}, u32[]{:S(2)}) copy-start(f32[27,32,4]{1,2,0:T(4,128)} %param.17) | copy-start | bytes 41476
  4.5 1.2 %copy-start.1 = (f32[1,4,4,128,128]{4,3,2,1,0:T(8,128)S(1)}, f32[1,4,4,128,128]{4,3,2,1,0:T(8,128)}, u32[]{:S(2)}) copy-start(f32[1,4,4,128,128]{4,3,2,1,0:T(8,128)} %param.11) | copy-start | bytes 3145732
